TPU v7x, 512 devices: a whole 4x4x16 slice. The times are simulated.
512 devices in a mesh: row: 16 (over x_hi, y, core), col: 32 (over x_lo, z).
Axes of the slice: x: 4 (x_hi: 2, x_lo: 2; x = x_hi * 2 + x_lo), y: 4, z: 16, core: 2. Of those that a mesh axis runs over, the one named last changes fastest.
Arguments:
- blocks: bfloat16 [1536, 64, 4096], P('col', 'row'), may hold values from -1.75 to 1.75
- columns: int32 [1536, 64], P('col', 'row'), may hold values from 0 to 95, as said below
- counts: int32 [1536, 16], P('col', 'row'), may hold values from 0 to 4, as said below
Outputs:
- product: bfloat16 [1536, 64, 4096], P('col', 'row')
Inputs may be any that keep to these rules, and one draw needn't show every extreme that they name: `counts`: in each tile, every block row has between 0 and 4 live slots; in every tile some block row has exactly 4. The live slots of a block row name different tile columns, at most 2 of them below 48 and at most 2 at or above; in every tile some block row reaches 2 in both halves. A live tile column t of global block row g satisfies (t - g) mod 48 < 8. Dead slots hold arbitrary values in the range.
All inputs are finite; a program needn't handle non-finite values.
Results may differ from a plain program's by a relative error of at most 0.001.
Values may be sent and summed in bfloat16 or wider, within the bound.
No kernel may reach another device: no remote copies, remote signals or barrier semaphores. Data moves between devices by JAX's collectives and lax.ppermute only.
A program may use at most 128 MiB of HBM per device.

v0:
```python
import jax
import jax.numpy as jnp
from jax import lax
from jax.sharding import PartitionSpec as P

BLK = 64
HS = 2
SECTIONS = 2


def broadcast(block, axis, owner):
    block = jnp.where(lax.axis_index(axis) == owner, block, jnp.zeros_like(block))
    return lax.psum(block, axis)


def from_behind(block, axis, distance):
    devices = range(lax.axis_size(axis))
    route = [((i - distance) % len(devices), i) for i in devices]
    return lax.ppermute(block, axis, route)


def compact(tile_blocks, tile_cols, tile_count, half_index):
    strip_count = tile_cols.shape[0]
    slot_count = tile_cols.shape[1]
    slot_ids = jnp.arange(slot_count, dtype=jnp.int32)
    live_slots = (slot_ids[None, :] < tile_count[:, None]) & (
        tile_cols // strip_count == half_index
    )
    position = jnp.cumsum(live_slots.astype(jnp.int32), axis=1) - 1
    chosen = live_slots[:, :, None] & (
        position[:, :, None] == jnp.arange(HS, dtype=jnp.int32)[None, None, :]
    )
    picked = jnp.einsum(
        "isq,isx->iqx",
        chosen.astype(jnp.bfloat16),
        tile_blocks,
        preferred_element_type=jnp.bfloat16,
    )
    inner_rows = jnp.sum(
        jnp.where(chosen, (tile_cols - half_index * strip_count)[:, :, None], 0), axis=1
    ).astype(jnp.int32)
    used_flags = jnp.any(chosen, axis=1).astype(jnp.int32)
    return (picked, inner_rows, used_flags)


def section_term(
    picked, inner_rows, used_flags, right_blocks, right_cols, right_count, out_cols, out_live
):
    strip_count = picked.shape[0]
    slot_count = out_cols.shape[1]
    gathered = right_blocks[inner_rows]
    gathered_cols = right_cols[inner_rows]
    gathered_count = right_count[inner_rows]
    slot_ids = jnp.arange(slot_count, dtype=jnp.int32)
    right_live = slot_ids[None, None, :] < gathered_count[:, :, None]
    matches = (gathered_cols[:, :, :, None] == out_cols[:, None, None, :]) & right_live[
        :, :, :, None
    ]
    matches = matches & (used_flags[:, :, None, None] > 0) & out_live[:, None, None, :]
    selected = jnp.einsum(
        "iqbj,iqbx->iqjx",
        matches.astype(jnp.bfloat16),
        gathered,
        preferred_element_type=jnp.bfloat16,
    )
    left_blocks = picked.reshape(strip_count, HS, BLK, BLK)
    right_sel = selected.reshape(strip_count, HS, slot_count, BLK, BLK)
    contribution = jnp.einsum(
        "iqmn,iqjnp->ijmp", left_blocks, right_sel, preferred_element_type=jnp.float32
    )
    return contribution.reshape(strip_count, slot_count, BLK * BLK)


def local(blocks, columns, counts):
    count_now = counts[:, 0]
    strip_count = columns.shape[0]
    slot_count = columns.shape[1]
    out_live = jnp.arange(slot_count, dtype=jnp.int32)[None, :] < count_now[:, None]
    col_index = lax.axis_index("col")
    col_total = lax.axis_size("col")
    accumulated = jnp.zeros((strip_count, slot_count, blocks.shape[2]), jnp.float32)
    right_tile = (blocks, columns, count_now)
    for section in range(SECTIONS):
        target_piece = (col_index + section) % col_total
        root_index = target_piece // 2
        half_index = target_piece % 2
        got_blocks, got_cols, got_count = (
            broadcast(blocks, "row", root_index),
            broadcast(columns, "row", root_index),
            broadcast(count_now, "row", root_index),
        )
        picked, inner_rows, used_flags = compact(got_blocks, got_cols, got_count, half_index)
        if section > 0:
            right_tile = from_behind((right_tile[0], right_tile[1], right_tile[2]), "col", -1)
        accumulated = accumulated + section_term(
            picked,
            inner_rows,
            used_flags,
            right_tile[0],
            right_tile[1],
            right_tile[2],
            columns,
            out_live,
        )
    return accumulated.astype(jnp.bfloat16)


def solution(mesh):
    return jax.shard_map(
        local,
        mesh=mesh,
        in_specs=(P("col", "row", None), P("col", "row"), P("col", "row")),
        out_specs=P("col", "row", None),
        check_vma=False,
    )
```

profile of v0, /device:TPU:1, one launch (start us, length us, event | category | flops | bytes accessed | tf_op | source)
XLA Modules:
  0.0 228.3 jit_solution(16284222606765548050)
XLA Ops:
  6.5 12.9 %collective-permute-start.2 = (bf16[48,4,4096]{2,1,0:T(4,128)(2,1)}, bf16[48,4,4096]{2,1,0:T(4,128)(2,1)S(1)}, u32[]{:S(2)}, u32[]{:S(2)}) collective-permute-start(bf16[48,4,4096]{2,1,0:T(4,128)(2,1)} %param.3), channel_id=1, source_target_pairs={{1,0},{2,1},{3,2},{4,3},{5,4},{6,5},{7,6},{8,7},{9,8},{10,9},{11,1... | collective-permute-start | bytes 4718600 | tf_op jit(solution)/shard_map/ppermute | solution.py:19
  19.4 0.8 copy.37
  20.2 2.6 %collective-permute-start = (s32[48,4]{1,0:T(8,128)S(1)}, s32[48,4]{1,0:T(8,128)S(1)}, u32[]{:S(2)}, u32[]{:S(2)}) collective-permute-start(s32[48,4]{1,0:T(8,128)S(1)} %copy.37), channel_id=1, source_target_pairs={{1,0},{2,1},{3,2},{4,3},{5,4},{6,5},{7,6},{8,7},{9,8},{10,9},{11,1... | collective-permute-start | bytes 2312 | tf_op jit(solution)/shard_map/ppermute | solution.py:19
  22.8 2.6 %collective-permute-start.1 = (s32[48]{0:T(128)}, s32[48]{0:T(128)S(1)}, u32[]{:S(2)}, u32[]{:S(2)}) collective-permute-start(s32[48]{0:T(128)} %bitcast.53), channel_id=1, source_target_pairs={{1,0},{2,1},{3,2},{4,3},{5,4},{6,5},{7,6},{8,7},{9,8},{10,9},{11,1... | collective-permute-start | bytes 584 | tf_op jit(solution)/shard_map/ppermute | solution.py:19
  25.5 0.0 copy-start.3
  25.6 0.0 copy-start.1
  25.6 4.4 %broadcast_select_fusion = (bf16[48,4,4096]{2,1,0:T(4,128)(2,1)}, bf16[48,4,4096]{2,1,0:T(4,128)(2,1)}) fusion(bf16[48,4,4096]{2,1,0:T(4,128)(2,1)} %param.3, pred[]{:T(512)S(6)} %eq.86, pred[]{:T(512)S(6)} %eq.39), kind=kLoop, calls=%fused_computation.12 | loop fusion | flops 1572864 | bytes 4718594 | tf_op jit(solution)/shard_map/jit(_where)/select_n | solution.py:12
  29.9 0.0 all-reduce.4.cloned.1.call-update
  30.0 12.7 %all-reduce = (s32[48,4]{0,1:T(4,128)S(1)}, s32[48]{0:T(128)S(1)}, s32[48,4]{0,1:T(4,128)S(1)}, s32[48]{0:T(128)S(1)}) all-reduce(s32[48,4]{0,1:T(4,128)S(1)} %get-tuple-element.22, s32[48]{0:T(128)S(1)} %get-tuple-element.24, s32[48,4]{0,1:T(4,128)S(1)} %get-tuple-element.21, ...), channel_id=1, replica_groups=mesh['row'=16,'col'=32] {'row'}, use_global_device_ids=true, to_apply=%region_1.2 | all-reduce | flops 480 | bytes 3840 | tf_op jit(solution)/shard_map/psum | solution.py:13
  42.9 0.1 copy.34
  43.0 0.1 copy.33
  43.1 0.1 copy.32
  43.2 0.1 copy.42
  43.3 0.1 copy.41
  43.4 1.7 fusion.31
  45.1 0.9 select_reduce_fusion.1
  46.0 0.1 copy.35
  46.1 0.1 copy.36
  46.2 0.1 reshape.107
  46.3 7.4 %gather_fusion.2 = bf16[96,4,4096]{2,1,0:T(4,128)(2,1)} fusion(bf16[48,4,4096]{2,1,0:T(4,128)(2,1)S(1)} %copy-done.1, s32[1024]{0:T(1024)S(1)} %pad_clamp_fusion.1), kind=kCustom, calls=%fused_computation.2 | custom fusion | bytes 6291840 | tf_op jit(solution)/shard_map/gather | solution.py:51
  53.7 0.6 gather_fusion
  54.3 1.2 gather_fusion.1
  55.5 0.1 reshape.114
  55.7 0.1 copy.43
  55.8 0.9 select_reduce_fusion
  56.7 0.1 copy.44
  56.7 0.1 copy.45
  56.8 0.1 reshape.131
  57.0 0.1 iota_compare_fusion.2
  57.1 0.1 iota_compare_fusion.1
  57.2 5.5 %fusion.10 = bf16[48,2,4,4096]{3,2,1,0:T(4,128)(2,1)} fusion(bf16[48,2,4,4096]{3,2,1,0:T(4,128)(2,1)} %bitcast.58, s32[48,4]{1,0:T(8,128)S(1)} %copy.37, s32[48,2,4]{2,1,0:T(2,128)S(1)} %bitcast.60, pred[48,4]{1,0:T(8,128)(4,1)S(1)} %iota_compare_fusion.2, pred[48,2]{1,0:T(8,128)(4,1)S(1)} %convert_compare_fusion.1, ...), kind=kOutput, calls=%fused_computation.19 | convolution fusion | flops 12589056 | bytes 6294432 | tf_op jit(solution)/shard_map/iqbj,iqbx->iqjx/dot_general | solution.py:60
  62.7 10.0 %reshape.101 = bf16[48,2,4,64,64]{4,3,2,1,0:T(8,128)(2,1)} reshape(bf16[48,2,4,4096]{3,2,1,0:T(4,128)(2,1)} %fusion.10) | data formatting | bytes 6291456 | tf_op jit(solution)/shard_map/reshape | solution.py:67
  72.7 1.2 gather_fusion.4
  74.0 0.1 reshape.138
  74.1 0.1 iota_compare_fusion
  74.2 0.6 gather_fusion.3
  74.9 7.3 %gather_fusion.5 = bf16[96,4,4096]{2,1,0:T(4,128)(2,1)} fusion(bf16[48,4,4096]{2,1,0:T(4,128)(2,1)S(1)} %collective-permute-done.2, s32[1024]{0:T(1024)S(1)} %pad_clamp_fusion), kind=kCustom, calls=%fused_computation.5 | custom fusion | bytes 6291840 | tf_op jit(solution)/shard_map/gather | solution.py:51
  82.1 5.5 %fusion.5 = bf16[48,2,4,4096]{3,2,1,0:T(4,128)(2,1)} fusion(bf16[48,2,4,4096]{3,2,1,0:T(4,128)(2,1)} %bitcast.59, s32[48,2,4]{2,1,0:T(2,128)S(1)} %bitcast.61, s32[48,4]{1,0:T(8,128)S(1)} %copy.37, pred[48,2]{1,0:T(8,128)(4,1)S(1)} %convert_compare_fusion, pred[48,2,4]{2,1,0:T(4,128)(4,1)S(1)} %iota_compare_fusion, pred[48,4]{1,0:T(8,128)(4,1)S(1)} %iota_compare_fusion.2), kind=kOutput, calls=%fused_computation.14 | convolution fusion | flops 12589056 | bytes 6294432 | tf_op jit(solution)/shard_map/iqbj,iqbx->iqjx/dot_general | solution.py:60
  87.6 10.0 %reshape.103 = bf16[48,2,4,64,64]{4,3,2,1,0:T(8,128)(2,1)} reshape(bf16[48,2,4,4096]{3,2,1,0:T(4,128)(2,1)} %fusion.5) | data formatting | bytes 6291456 | tf_op jit(solution)/shard_map/reshape | solution.py:67
  97.6 94.2 %all-reduce.4.cloned.1.call-done = (bf16[48,4,4096]{2,1,0:T(4,128)(2,1)}, bf16[48,4,4096]{2,1,0:T(4,128)(2,1)}) async-done(((bf16[48,4,4096]{2,1,0:T(4,128)(2,1)}, bf16[48,4,4096]{2,1,0:T(4,128)(2,1)}), (bf16[48,4,4096]{2,1,0:T(4,128)(2,1)}, bf16[48,4,4096]{2,1,0:T(4,128)(2,1)})) %all-reduce.4.cloned.1.call-update) | async-done | bytes 3145744 | tf_op jit(solution)/shard_map/psum | solution.py:13
  191.8 2.4 %fusion.37 = bf16[48,2,4096]{2,1,0:T(2,128)(2,1)S(1)} fusion(pred[48,4,2]{1,2,0:T(4,128)(4,1)S(1)} %get-tuple-element.26, bf16[48,4,4096]{2,1,0:T(4,128)(2,1)} %get-tuple-element.9), kind=kOutput, calls=%fused_computation.73 | convolution fusion | flops 3145728 | bytes 2359680 | tf_op jit(solution)/shard_map/isq,isx->iqx/dot_general | solution.py:33
  194.2 1.9 reshape.159
  196.1 2.4 %fusion.38 = bf16[48,2,4096]{2,1,0:T(2,128)(2,1)S(1)} fusion(pred[48,4,2]{1,2,0:T(4,128)(4,1)S(1)} %get-tuple-element.12, bf16[48,4,4096]{2,1,0:T(4,128)(2,1)} %get-tuple-element.10), kind=kOutput, calls=%fused_computation.74 | convolution fusion | flops 3145728 | bytes 2359680 | tf_op jit(solution)/shard_map/isq,isx->iqx/dot_general | solution.py:33
  198.5 1.9 reshape.161
  200.4 7.8 %fusion.3 = f32[48,4,64,64,1]{3,2,1,4,0:T(8,128)} fusion(bf16[48,2,4,64,64]{4,3,2,1,0:T(8,128)(2,1)} %reshape.101, bf16[48,2,64,64,1]{3,2,1,0,4:T(8,128)(2,1)} %reshape.159), kind=kOutput, calls=%fused_computation.10 | convolution fusion | flops 201326592 | bytes 7077888 | tf_op jit(solution)/shard_map/iqmn,iqjnp->ijmp/dot_general | solution.py:68
  208.3 6.5 %fusion.1 = bf16[48,4,64,64]{2,3,1,0:T(8,128)(2,1)} fusion(f32[48,4,64,64,1]{3,2,1,4,0:T(8,128)} %fusion.3, bf16[48,2,4,64,64]{4,3,2,1,0:T(8,128)(2,1)S(1)} %bitcast.57, bf16[48,2,64,64,1]{3,2,1,0,4:T(8,128)(2,1)S(1)} %copy-done.2), kind=kOutput, calls=%fused_computation.8 | convolution fusion | flops 202899456 | bytes 8650752 | tf_op jit(solution)/shard_map/iqmn,iqjnp->ijmp/dot_general | solution.py:68
  214.8 3.4 %copy.57 = bf16[48,4,64,64]{3,2,1,0:T(8,128)(2,1)S(1)} copy(bf16[48,4,64,64]{2,3,1,0:T(8,128)(2,1)} %fusion.1) | data formatting | bytes 3145728 | tf_op jit(solution)/shard_map/convert_element_type | solution.py:105
  218.2 3.2 %reshape.165 = bf16[48,4,4096]{2,1,0:T(4,128)(2,1)} reshape(bf16[48,4,64,64]{3,2,1,0:T(8,128)(2,1)S(1)} %copy.57) | data formatting | bytes 3145728 | tf_op jit(solution)/shard_map/convert_element_type | solution.py:105
  (30 shorter events, 0.2 us)
Async XLA Ops:
  6.5 185.3 %all-reduce.4.cloned.1.call-start = ((), (), s32[]{:S(2)}) async-start(), calls=%async_computation | async-start | bytes 6291456 | tf_op jit(solution)/shard_map/psum | solution.py:13
  6.5 68.3 %collective-permute-start.2 = (bf16[48,4,4096]{2,1,0:T(4,128)(2,1)}, bf16[48,4,4096]{2,1,0:T(4,128)(2,1)S(1)}, u32[]{:S(2)}, u32[]{:S(2)}) collective-permute-start(bf16[48,4,4096]{2,1,0:T(4,128)(2,1)} %param.3), channel_id=1, source_target_pairs={{1,0},{2,1},{3,2},{4,3},{5,4},{6,5},{7,6},{8,7},{9,8},{10,9},{11,1... | collective-permute-start | bytes 4718600 | tf_op jit(solution)/shard_map/ppermute | solution.py:19
  20.2 54.0 %collective-permute-start = (s32[48,4]{1,0:T(8,128)S(1)}, s32[48,4]{1,0:T(8,128)S(1)}, u32[]{:S(2)}, u32[]{:S(2)}) collective-permute-start(s32[48,4]{1,0:T(8,128)S(1)} %copy.37), channel_id=1, source_target_pairs={{1,0},{2,1},{3,2},{4,3},{5,4},{6,5},{7,6},{8,7},{9,8},{10,9},{11,1... | collective-permute-start | bytes 2312 | tf_op jit(solution)/shard_map/ppermute | solution.py:19
  22.8 49.9 %collective-permute-start.1 = (s32[48]{0:T(128)}, s32[48]{0:T(128)S(1)}, u32[]{:S(2)}, u32[]{:S(2)}) collective-permute-start(s32[48]{0:T(128)} %bitcast.53), channel_id=1, source_target_pairs={{1,0},{2,1},{3,2},{4,3},{5,4},{6,5},{7,6},{8,7},{9,8},{10,9},{11,1... | collective-permute-start | bytes 584 | tf_op jit(solution)/shard_map/ppermute | solution.py:19
  25.5 4.4 %copy-start = (s32[48,1]{0,1:T(1,128)S(1)}, s32[48,1]{0,1:T(1,128)}, u32[]{:S(2)}) copy-start(s32[48,1]{0,1:T(1,128)} %param.5) | copy-start | bytes 580
  25.5 4.4 %copy-start.3 = (s32[48,4]{0,1:T(4,128)S(1)}, s32[48,4]{0,1:T(4,128)}, u32[]{:S(2)}) copy-start(s32[48,4]{0,1:T(4,128)} %param.4) | copy-start | bytes 2308
  25.6 20.8 %copy-start.1 = (bf16[48,4,4096]{2,1,0:T(4,128)(2,1)S(1)}, bf16[48,4,4096]{2,1,0:T(4,128)(2,1)}, u32[]{:S(2)}) copy-start(bf16[48,4,4096]{2,1,0:T(4,128)(2,1)} %param.3) | copy-start | bytes 4718596
  198.5 9.8 %slice-start = ((s8[6291456]{0:T(1024)(128)(4,1)}), s8[2097152]{0:T(1024)(128)(4,1)S(1)}, s32[]{:S(2)}) async-start(s8[6291456]{0:T(1024)(128)(4,1)} %bitcast.56), calls=%async_computation.1 | async-start | bytes 4194304
  200.4 7.9 %slice-start.1 = ((s8[6291456]{0:T(1024)(128)(4,1)}), s8[4194304]{0:T(1024)(128)(4,1)S(1)}, s32[]{:S(2)}) async-start(s8[6291456]{0:T(1024)(128)(4,1)} %bitcast.56), calls=%async_computation.2 | async-start | bytes 8388608
  200.4 7.9 %copy-start.2 = (bf16[48,2,64,64,1]{3,2,1,0,4:T(8,128)(2,1)S(1)}, bf16[48,2,64,64,1]{3,2,1,0,4:T(8,128)(2,1)}, u32[]{:S(2)}) copy-start(bf16[48,2,64,64,1]{3,2,1,0,4:T(8,128)(2,1)} %reshape.161) | copy-start | bytes 2359300
Sparse Core Ops, SparseCore 0:
  30.1 161.6 all-reduce.3
where the time goes:
time: 229 us; the launch traced here: 228 us
  waiting for transfers between devices  94.2 us (41%)
  local copies, waits for them, and re-layouts  51 us (22%)
  matrix products  30.1 us (13%)
  starting transfers between devices  18.1 us (8%)
  between operations  13.7 us (6%)
  blocking collectives  12.7 us (6%)
  other arithmetic  8.37 us (4%)
    psum x1, waiting for transfers between devices, broadcast(): return lax.psum(block, axis)  94.2 us
    reshape x2, local copies, waits for them, and re-layouts, section_term(): right_sel = selected.reshape(strip_count, HS, slot_count, BLK, BLK)  20 us
    ppermute x3, starting transfers between devices, from_behind(): return lax.ppermute(block, axis, route)  18.1 us
    gather x2, local copies, waits for them, and re-layouts, section_term(): gathered = right_blocks[inner_rows]  14.6 us
    dot_general x2, matrix products, section_term(): jnp.einsum('iqmn,iqjnp->ijmp', left_blocks, right_sel, preferred_element_...  14.4 us
    psum x1, blocking collectives, broadcast(): return lax.psum(block, axis)  12.7 us
    dot_general x2, matrix products, section_term(): jnp.einsum('iqbj,iqbx->iqjx', matches.astype(jnp.bfloat16), gathered, pre...  11 us
    convert_element_type x2, local copies, waits for them, and re-layouts, local(): return accumulated.astype(jnp.bfloat16)  6.61 us
  transfers between devices with their start and end apart: 4, of which 1 were waited for; matrix products, arithmetic and copies ran while one was open for 26% of the time, Pallas kernels for 0%

commit v1 on v0

--- a/solution.py
+++ b/solution.py
@@ -10,7 +10,7 @@
 
 def broadcast(block, axis, owner):
     block = jnp.where(lax.axis_index(axis) == owner, block, jnp.zeros_like(block))
-    return lax.psum(block, axis)
+    return jnp.sum(lax.all_gather(block, axis), axis=0)
 
 
 def from_behind(block, axis, distance):

time: 229 us -> 409 us (1.79)
  waiting for transfers between devices: 94.2 us -> 202 us
  blocking collectives: 12.7 us -> 55.9 us
  other arithmetic: 8.37 us -> 35.6 us
    all_gather x0 -> x2, waiting for transfers between devices: none -> 202 us  [broadcast(): return jnp.sum(lax.all_gather(block, axis), axis=0)]
    psum x1 -> x0, waiting for transfers between devices: 94.2 us -> none  [broadcast(): return lax.psum(block, axis)]
    all_gather x0 -> x2, blocking collectives: none -> 42.5 us  [broadcast(): return jnp.sum(lax.all_gather(block, axis), axis=0)]
    reduce_sum x0 -> x6, other arithmetic: none -> 26.9 us  [broadcast(): return jnp.sum(lax.all_gather(block, axis), axis=0)]
    unnamed x0 -> x1, blocking collectives: none -> 13.4 us
    psum x1 -> x0, blocking collectives: 12.7 us -> none  [broadcast(): return lax.psum(block, axis)]
  transfers between devices with their start and end apart: 4 -> 5, of which waited for: 1 -> 2; matrix products, arithmetic and copies ran while one was open for 26% -> 17% of each run, Pallas kernels for 0% -> 0%
where the time goes in v1:
time: 409 us; the launch traced here: 408 us
  waiting for transfers between devices  202 us (49%)
  blocking collectives  55.9 us (14%)
  local copies, waits for them, and re-layouts  53.4 us (13%)
  other arithmetic  35.6 us (9%)
  matrix products  28.4 us (7%)
  starting transfers between devices  18.2 us (4%)
  between operations  14.3 us (3%)
    all_gather x2, waiting for transfers between devices, broadcast(): return jnp.sum(lax.all_gather(block, axis), axis=0)  202 us
    all_gather x2, blocking collectives, broadcast(): return jnp.sum(lax.all_gather(block, axis), axis=0)  42.5 us
    reduce_sum x6, other arithmetic, broadcast(): return jnp.sum(lax.all_gather(block, axis), axis=0)  26.9 us
    reshape x2, local copies, waits for them, and re-layouts, section_term(): right_sel = selected.reshape(strip_count, HS, slot_count, BLK, BLK)  20.2 us
    ppermute x3, starting transfers between devices, from_behind(): return lax.ppermute(block, axis, route)  18.1 us
    dot_general x2, matrix products, section_term(): jnp.einsum('iqmn,iqjnp->ijmp', left_blocks, right_sel, preferred_element_...  14.5 us
    gather x2, local copies, waits for them, and re-layouts, section_term(): gathered = right_blocks[inner_rows]  14.3 us
    unnamed x1, blocking collectives  13.4 us
  transfers between devices with their start and end apart: 5, of which 2 were waited for; matrix products, arithmetic and copies ran while one was open for 17% of the time, Pallas kernels for 0%

profile of v1, /device:TPU:1, one launch (start us, length us, event | category | flops | bytes accessed | tf_op | source)
XLA Modules:
  0.0 408.0 jit_solution(419938740897597998)
XLA Ops:
  6.5 4.4 %broadcast_select_fusion = (bf16[48,4,4096]{2,1,0:T(4,128)(2,1)}, bf16[48,4,4096]{2,1,0:T(4,128)(2,1)}) fusion(bf16[48,4,4096]{2,1,0:T(4,128)(2,1)} %param.3, pred[]{:T(512)S(6)} %eq.102, pred[]{:T(512)S(6)} %eq.93), kind=kLoop, calls=%fused_computation.12 | loop fusion | flops 1572864 | bytes 4718594 | tf_op jit(solution)/shard_map/jit(_where)/select_n | solution.py:12
  11.0 0.7 all-gather.11.cloned.1.call-update
  11.7 12.9 %collective-permute-start.2 = (bf16[48,4,4096]{2,1,0:T(4,128)(2,1)S(1)}, bf16[48,4,4096]{2,1,0:T(4,128)(2,1)S(1)}, u32[]{:S(2)}, u32[]{:S(2)}) collective-permute-start(bf16[48,4,4096]{2,1,0:T(4,128)(2,1)S(1)} %copy-done.1), channel_id=1, source_target_pairs={{1,0},{2,1},{3,2},{4,3},{5,4},{6,5},{7,6},{8,7},{9,8},{10,9},{11,1... | collective-permute-start | bytes 4718600 | tf_op jit(solution)/shard_map/ppermute | solution.py:19
  24.6 2.6 collective-permute-start.1
  27.3 2.6 collective-permute-start
  30.0 1.3 dynamic-slice
  31.9 0.1 fusion.32
  32.1 13.4 %all-reduce.2 = (s32[768]{0:T(1024)S(1)}, s32[768]{0:T(1024)S(1)}) all-reduce(s32[768]{0:T(1024)S(1)} %fusion.32, s32[768]{0:T(1024)S(1)} %fusion.34), channel_id=2, replica_groups=mesh['row'=16,'col'=32] {'row'}, use_global_device_ids=true, to_apply=%add | all-reduce | flops 1536 | bytes 12288
  45.6 22.4 %all-gather.6 = s32[16,48,4]{1,2,0:T(4,128)S(1)} all-gather(s32[1,48,4]{1,2,0:T(4,128)S(1)} %get-tuple-element.18), channel_id=3, replica_groups=mesh['row'=16,'col'=32] {'row'}, dimensions={0}, use_global_device_ids=true | all-gather | bytes 13056 | tf_op jit(solution)/shard_map/all_gather | solution.py:13
  68.0 0.1 copy.49
  68.2 0.1 copy.50
  68.3 0.1 copy.51
  68.4 0.9 fusion.38
  69.3 0.9 select_reduce_fusion.1
  70.3 0.1 copy.53
  70.3 0.1 reshape.257
  70.5 1.2 gather_fusion.1
  71.7 0.6 gather_fusion
  72.4 7.2 %gather_fusion.2 = bf16[96,4,4096]{2,1,0:T(4,128)(2,1)} fusion(bf16[48,4,4096]{2,1,0:T(4,128)(2,1)S(1)} %copy-done.1, s32[1024]{0:T(1024)S(1)} %pad_clamp_fusion.1), kind=kCustom, calls=%fused_computation.2 | custom fusion | bytes 6291840 | tf_op jit(solution)/shard_map/gather | solution.py:51
  79.6 20.1 %all-gather.7 = s32[16,48,4]{1,2,0:T(4,128)S(1)} all-gather(s32[1,48,4]{1,2,0:T(4,128)S(1)} %get-tuple-element.17), channel_id=6, replica_groups=mesh['row'=16,'col'=32] {'row'}, dimensions={0}, use_global_device_ids=true | all-gather | bytes 13056 | tf_op jit(solution)/shard_map/all_gather | solution.py:13
  99.8 0.1 copy.58
  99.9 0.1 copy.59
  100.1 0.9 fusion.35
  101.0 0.9 select_reduce_fusion
  102.1 0.1 reshape.281
  102.2 0.1 reshape.264
  102.5 0.1 iota_compare_fusion.1
  102.6 5.7 %fusion.10 = bf16[48,2,4,4096]{3,2,1,0:T(4,128)(2,1)} fusion(bf16[48,2,4,4096]{3,2,1,0:T(4,128)(2,1)} %bitcast.73, s32[48,4]{1,0:T(8,128)S(1)} %copy.54, s32[48,2,4]{2,1,0:T(2,128)S(1)} %bitcast.75, pred[48,4]{1,0:T(8,128)(4,1)S(1)} %iota_compare_fusion.2, pred[48,2]{1,0:T(8,128)(4,1)S(1)} %convert_compare_fusion.1, ...), kind=kOutput, calls=%fused_computation.19 | convolution fusion | flops 12589056 | bytes 6294432 | tf_op jit(solution)/shard_map/iqbj,iqbx->iqjx/dot_general | solution.py:60
  108.3 10.2 %reshape.251 = bf16[48,2,4,64,64]{4,3,2,1,0:T(8,128)(2,1)} reshape(bf16[48,2,4,4096]{3,2,1,0:T(4,128)(2,1)} %fusion.10) | data formatting | bytes 6291456 | tf_op jit(solution)/shard_map/reshape | solution.py:67
  118.5 1.2 gather_fusion.4
  119.7 0.1 reshape.288
  119.8 0.1 iota_compare_fusion
  120.0 0.6 gather_fusion.3
  120.6 7.2 %gather_fusion.5 = bf16[96,4,4096]{2,1,0:T(4,128)(2,1)} fusion(bf16[48,4,4096]{2,1,0:T(4,128)(2,1)S(1)} %collective-permute-done.2, s32[1024]{0:T(1024)S(1)} %pad_clamp_fusion), kind=kCustom, calls=%fused_computation.5 | custom fusion | bytes 6291840 | tf_op jit(solution)/shard_map/gather | solution.py:51
  127.8 5.4 %fusion.5 = bf16[48,2,4,4096]{3,2,1,0:T(4,128)(2,1)} fusion(bf16[48,2,4,4096]{3,2,1,0:T(4,128)(2,1)} %bitcast.74, s32[48,2,4]{2,1,0:T(2,128)S(1)} %bitcast.76, s32[48,4]{1,0:T(8,128)S(1)} %copy.54, pred[48,2]{1,0:T(8,128)(4,1)S(1)} %convert_compare_fusion, pred[48,2,4]{2,1,0:T(4,128)(4,1)S(1)} %iota_compare_fusion, pred[48,4]{1,0:T(8,128)(4,1)S(1)} %iota_compare_fusion.2), kind=kOutput, calls=%fused_computation.14 | convolution fusion | flops 12589056 | bytes 6294432 | tf_op jit(solution)/shard_map/iqbj,iqbx->iqjx/dot_general | solution.py:60
  133.2 10.0 %reshape.253 = bf16[48,2,4,64,64]{4,3,2,1,0:T(8,128)(2,1)} reshape(bf16[48,2,4,4096]{3,2,1,0:T(4,128)(2,1)} %fusion.5) | data formatting | bytes 6291456 | tf_op jit(solution)/shard_map/reshape | solution.py:67
  143.2 51.8 %all-gather.13.cloned.1.call-done = bf16[768,4,4096]{2,1,0:T(4,128)(2,1)} async-done(((bf16[48,4,4096]{2,1,0:T(4,128)(2,1)}), bf16[768,4,4096]{2,1,0:T(4,128)(2,1)}) %all-gather.13.cloned.1.call-update) | async-done | bytes 25165840 | tf_op jit(solution)/shard_map/all_gather | solution.py:13
  195.0 13.3 %reduce_sum.91 = bf16[48,4,4096]{2,1,0:T(4,128)(2,1)S(1)} reduce(bf16[16,48,4,4096]{3,2,1,0:T(4,128)(2,1)} %bitcast.69, bf16[]{:T(256)} %constant.89.clone.1), dimensions={0}, to_apply=%region_11.12 | reduce | flops 11796480 | bytes 26738690 | tf_op jit(solution)/shard_map/reduce_sum | solution.py:13
  208.3 1.0 fusion.42
  209.3 149.8 %all-gather.11.cloned.1.call-done = bf16[768,4,4096]{2,1,0:T(4,128)(2,1)} async-done(((bf16[48,4,4096]{2,1,0:T(4,128)(2,1)}), bf16[768,4,4096]{2,1,0:T(4,128)(2,1)}) %all-gather.11.cloned.1.call-update) | async-done | bytes 25165840 | tf_op jit(solution)/shard_map/all_gather | solution.py:13
  359.0 13.5 %reduce_sum.86 = bf16[48,4,4096]{2,1,0:T(4,128)(2,1)S(1)} reduce(bf16[16,48,4,4096]{3,2,1,0:T(4,128)(2,1)} %bitcast.70, bf16[]{:T(256)} %constant.89.clone.1), dimensions={0}, to_apply=%region_5.6 | reduce | flops 11796480 | bytes 26738690 | tf_op jit(solution)/shard_map/reduce_sum | solution.py:13
  372.6 1.8 fusion.41
  374.4 3.8 reshape.333
  378.2 1.9 reshape.335
  380.1 7.9 %fusion.3 = f32[48,4,64,64,1]{3,2,1,4,0:T(8,128)} fusion(bf16[48,2,4,64,64]{4,3,2,1,0:T(8,128)(2,1)} %reshape.251, bf16[48,2,64,64,1]{3,2,1,0,4:T(8,128)(2,1)} %reshape.333), kind=kOutput, calls=%fused_computation.10 | convolution fusion | flops 201326592 | bytes 7077888 | tf_op jit(solution)/shard_map/iqmn,iqjnp->ijmp/dot_general | solution.py:68
  388.0 6.6 %fusion.1 = bf16[48,4,64,64]{2,3,1,0:T(8,128)(2,1)} fusion(f32[48,4,64,64,1]{3,2,1,4,0:T(8,128)} %fusion.3, bf16[48,2,4,64,64]{4,3,2,1,0:T(8,128)(2,1)S(1)} %bitcast.72, bf16[48,2,64,64,1]{3,2,1,0,4:T(8,128)(2,1)S(1)} %copy-done.2), kind=kOutput, calls=%fused_computation.8 | convolution fusion | flops 202899456 | bytes 8650752 | tf_op jit(solution)/shard_map/iqmn,iqjnp->ijmp/dot_general | solution.py:68
  394.6 3.4 copy.74
  398.0 3.2 reshape.339
  (49 shorter events, 1.1 us)
Async XLA Ops:
  6.5 188.4 %all-gather.13.cloned.1.call-start = ((), (), s32[]{:S(2)}) async-start(), calls=%async_computation.1 | async-start | bytes 26738688 | tf_op jit(solution)/shard_map/all_gather | solution.py:13
  6.5 5.1 %copy-start.1 = (bf16[48,4,4096]{2,1,0:T(4,128)(2,1)S(1)}, bf16[48,4,4096]{2,1,0:T(4,128)(2,1)}, u32[]{:S(2)}) copy-start(bf16[48,4,4096]{2,1,0:T(4,128)(2,1)} %param.3) | copy-start | bytes 4718596
  6.5 18.0 %copy-start = (s32[48,1]{0,1:T(1,128)S(1)}, s32[48,1]{0,1:T(1,128)}, u32[]{:S(2)}) copy-start(s32[48,1]{0,1:T(1,128)} %param.5) | copy-start | bytes 580
  6.5 20.7 %copy-start.3 = (s32[48,4]{0,1:T(4,128)S(1)}, s32[48,4]{0,1:T(4,128)}, u32[]{:S(2)}) copy-start(s32[48,4]{0,1:T(4,128)} %param.4) | copy-start | bytes 2308
  10.9 348.1 %all-gather.11.cloned.1.call-start = ((), (), s32[]{:S(2)}) async-start(), calls=%async_computation | async-start | bytes 26738688 | tf_op jit(solution)/shard_map/all_gather | solution.py:13
  11.7 108.9 %collective-permute-start.2 = (bf16[48,4,4096]{2,1,0:T(4,128)(2,1)S(1)}, bf16[48,4,4096]{2,1,0:T(4,128)(2,1)S(1)}, u32[]{:S(2)}, u32[]{:S(2)}) collective-permute-start(bf16[48,4,4096]{2,1,0:T(4,128)(2,1)S(1)} %copy-done.1), channel_id=1, source_target_pairs={{1,0},{2,1},{3,2},{4,3},{5,4},{6,5},{7,6},{8,7},{9,8},{10,9},{11,1... | collective-permute-start | bytes 4718600 | tf_op jit(solution)/shard_map/ppermute | solution.py:19
  24.6 93.9 %collective-permute-start.1 = (s32[48]{0:T(128)S(1)}, s32[48]{0:T(128)S(1)}, u32[]{:S(2)}, u32[]{:S(2)}) collective-permute-start(s32[48]{0:T(128)S(1)} %bitcast.66), channel_id=1, source_target_pairs={{1,0},{2,1},{3,2},{4,3},{5,4},{6,5},{7,6},{8,7},{9,8},{10,9},{11,1... | collective-permute-start | bytes 584 | tf_op jit(solution)/shard_map/ppermute | solution.py:19
  27.3 92.6 %collective-permute-start = (s32[48,4]{1,0:T(8,128)S(1)}, s32[48,4]{1,0:T(8,128)S(1)}, u32[]{:S(2)}, u32[]{:S(2)}) collective-permute-start(s32[48,4]{1,0:T(8,128)S(1)} %copy.54), channel_id=1, source_target_pairs={{1,0},{2,1},{3,2},{4,3},{5,4},{6,5},{7,6},{8,7},{9,8},{10,9},{11,1... | collective-permute-start | bytes 2312 | tf_op jit(solution)/shard_map/ppermute | solution.py:19
  378.2 9.8 %slice-start = ((s8[6291456]{0:T(1024)(128)(4,1)}), s8[2097152]{0:T(1024)(128)(4,1)S(1)}, s32[]{:S(2)}) async-start(s8[6291456]{0:T(1024)(128)(4,1)} %bitcast.71), calls=%async_computation.2 | async-start | bytes 4194304
  380.1 7.9 %slice-start.1 = ((s8[6291456]{0:T(1024)(128)(4,1)}), s8[4194304]{0:T(1024)(128)(4,1)S(1)}, s32[]{:S(2)}) async-start(s8[6291456]{0:T(1024)(128)(4,1)} %bitcast.71), calls=%async_computation.3 | async-start | bytes 8388608
  380.1 7.9 %copy-start.2 = (bf16[48,2,64,64,1]{3,2,1,0,4:T(8,128)(2,1)S(1)}, bf16[48,2,64,64,1]{3,2,1,0,4:T(8,128)(2,1)}, u32[]{:S(2)}) copy-start(bf16[48,2,64,64,1]{3,2,1,0,4:T(8,128)(2,1)} %reshape.335) | copy-start | bytes 2359300
Sparse Core Ops, SparseCore 0:
  11.1 183.8 all-gather.12
  198.3 160.6 all-gather.10
